TPU v7x, 512 devices: a whole 4x8x8 slice. The times are simulated.
512 devices in a mesh: dp: 16 (over x_lo, z), fsdp: 32 (over x_hi, y, core).
Axes of the slice: x: 4 (x_hi: 2, x_lo: 2; x = x_hi * 2 + x_lo), y: 8, z: 8, core: 2. Of those that a mesh axis runs over, the one named last changes fastest.
Arguments:
- layer_input: bfloat16 [32768, 8192], P('dp', 'fsdp'), may hold values from -6 to 6
- cotangent: bfloat16 [2, 32768, 1024], P(None, ('dp', 'fsdp')), may hold values from -6 to 6
- candidates: bfloat16 [2, 16, 1024, 512], P(None, 'dp', None, 'fsdp'), may hold values from -0.1875 to 0.1875
- moment_first: float32 [2, 512, 8192], P(None, 'dp', 'fsdp'), may hold values from -0.6 to 0.6
- moment_second: float32 [2, 512, 8192], P(None, 'dp', 'fsdp'), may hold values from 0.0001 to 0.01
- owners: int32 [2], replicated, may hold values from 0 to 15
Outputs:
- update: bfloat16 [2, 1024, 8192], P(None, 'dp', 'fsdp')
- first_next: float32 [2, 512, 8192], P(None, 'dp', 'fsdp')
- second_next: float32 [2, 512, 8192], P(None, 'dp', 'fsdp')
Inputs may be any that keep to these rules, and one draw needn't show every extreme that they name: owners[m] names a data-parallel replica.
All inputs are finite; a program needn't handle non-finite values.
Results may differ from a plain program's by a relative error of at most 0.0056.
Values may be sent and summed in bfloat16 or wider, within the bound.
A program may use at most 64 MiB of HBM per device.

v0:
```python
import math
import jax
import jax.numpy as jnp
from jax import lax
from jax.sharding import PartitionSpec as P

MATS = 2
STEP = 10
beta_first = 0.9
beta_second = 0.999
epsilon = 1e-08


def broadcast(x, axis, root):
    return lax.dynamic_index_in_dim(lax.all_gather(x, axis), root, 0, keepdims=False)


def sent_to_all(x, axis):
    count = lax.axis_size(axis)
    return lax.all_to_all(jnp.broadcast_to(x[None], (count, *x.shape)), axis, 0, 0, tiled=True)


def in_order(blocks, dim):
    lengths = list(blocks.shape[1:])
    lengths[dim] *= blocks.shape[0]
    return jnp.moveaxis(blocks, 0, dim).reshape(lengths)


def collect(x, axis, dim):
    blocks = sent_to_all(x, axis)
    return in_order(blocks, dim)


def cut_along(x, dim, count):
    before, after = (x.shape[:dim], x.shape[dim + 1 :])
    return jnp.moveaxis(x.reshape(*before, count, -1, *after), dim, 0)


def summed_on_arrival(x, axis, dim):
    blocks = cut_along(x, dim, lax.axis_size(axis))
    arrived = lax.all_to_all(blocks, axis, split_axis=0, concat_axis=0, tiled=True)
    return arrived.sum(axis=0)


def on_device(layer_input, cotangent, candidates, moment_first, moment_second, owners):
    replicas = lax.axis_size("dp")
    replica_index = lax.axis_index("dp")
    inverse_root = 1.0 / math.sqrt(layer_input.shape[0] * replicas)
    kv_share = candidates.shape[2] // replicas
    updates = []
    firsts = []
    seconds = []
    for matrix in range(MATS):
        candidate_own = candidates[matrix, 0]
        owner_index = owners[matrix]
        owner_block = broadcast(candidate_own, "dp", owner_index)
        projector = collect(owner_block, "fsdp", 1)
        head_rows = jnp.dot(
            cotangent[matrix], projector, preferred_element_type=jnp.float32
        ).astype(jnp.bfloat16)
        partial_value = lax.dot_general(
            lax.all_gather(head_rows, "fsdp", axis=0, tiled=True),
            layer_input,
            (((0,), (0,)), ((), ())),
            preferred_element_type=jnp.float32,
        )
        projected = summed_on_arrival(partial_value, "dp", 0) * inverse_root
        first = beta_first * moment_first[matrix] + (1.0 - beta_first) * projected
        second = beta_second * moment_second[matrix] + (1.0 - beta_second) * projected * projected
        direction = (
            first
            / (1.0 - beta_first**STEP)
            / (jnp.sqrt(second / (1.0 - beta_second**STEP)) + epsilon)
        )
        direction = direction.astype(jnp.bfloat16)
        own_rows = lax.dynamic_slice_in_dim(projector, replica_index * kv_share, kv_share, 0)
        update = jnp.dot(own_rows, collect(direction, "dp", 0), preferred_element_type=jnp.float32)
        updates.append(update.astype(jnp.bfloat16))
        firsts.append(first)
        seconds.append(second)
    return (jnp.stack(updates), jnp.stack(firsts), jnp.stack(seconds))


def solution(mesh):
    placed = (
        P("dp", "fsdp"),
        P(None, ("dp", "fsdp"), None),
        P(None, "dp", None, "fsdp"),
        P(None, "dp", "fsdp"),
        P(None, "dp", "fsdp"),
        P(),
    )
    return jax.shard_map(
        on_device,
        mesh=mesh,
        in_specs=placed,
        out_specs=(P(None, "dp", "fsdp"), P(None, "dp", "fsdp"), P(None, "dp", "fsdp")),
        check_vma=False,
    )
```

profile of v0, /device:TPU:2, one launch (start us, length us, event | category | flops | bytes accessed | tf_op | source)
XLA Modules:
  0.0 325.7 jit_solution(12973515239512783485)
XLA Ops:
  7.2 0.0 all-gather.7.cloned.1.call-start
  7.2 1.4 fusion.15
  9.9 0.8 fusion.14
  10.7 41.3 %all-gather.1 = bf16[16,1,1024,16]{2,3,1,0:T(8,128)(2,1)S(1)} all-gather(bf16[1,1,1024,16]{2,3,1,0:T(8,128)(2,1)S(1)} %get-tuple-element.13), channel_id=3, replica_groups=mesh['dp'=16,'fsdp'=32] {'dp'}, dimensions={0}, use_global_device_ids=true | all-gather | bytes 557056 | tf_op jit(solution)/shard_map/all_gather | solution.py:15
  52.6 0.1 broadcast_in_dim.37
  52.8 39.1 %all_to_all.30 = bf16[32,1024,16]{1,2,0:T(8,128)(2,1)S(1)} all-to-all(bf16[32,1024,16]{1,2,0:T(8,128)(2,1)S(1)} %broadcast_in_dim.37), channel_id=1, replica_groups=mesh['dp'=16,'fsdp'=32] {'fsdp'}, dimensions={0} | all-to-all | bytes 2097152 | tf_op jit(solution)/shard_map/all_to_all | solution.py:20
  91.9 1.1 fusion.1
  93.0 0.0 all-gather.7.cloned.1.call-update
  93.0 0.0 all-gather.5.cloned.1.call-start
  95.0 33.0 %all-gather = bf16[16,1,1024,16]{2,3,1,0:T(8,128)(2,1)S(1)} all-gather(bf16[1,1,1024,16]{2,3,1,0:T(8,128)(2,1)S(1)} %get-tuple-element.12), channel_id=2, replica_groups=mesh['dp'=16,'fsdp'=32] {'dp'}, dimensions={0}, use_global_device_ids=true | all-gather | bytes 557056 | tf_op jit(solution)/shard_map/all_gather | solution.py:15
  128.0 0.1 broadcast_in_dim.33
  128.1 37.3 %all_to_all.31 = bf16[32,1024,16]{1,2,0:T(8,128)(2,1)S(1)} all-to-all(bf16[32,1024,16]{1,2,0:T(8,128)(2,1)S(1)} %broadcast_in_dim.33), channel_id=1, replica_groups=mesh['dp'=16,'fsdp'=32] {'fsdp'}, dimensions={0} | all-to-all | bytes 2097152 | tf_op jit(solution)/shard_map/all_to_all | solution.py:20
  165.4 1.1 fusion
  166.5 0.0 all-gather.5.cloned.1.call-update
  166.5 7.0 %all-gather.7.cloned.1.call-done = bf16[2048,512]{1,0:T(8,128)(2,1)} async-done(((bf16[64,512]{1,0:T(8,128)(2,1)}), bf16[2048,512]{1,0:T(8,128)(2,1)}) %all-gather.7.cloned.1.call-update) | async-done | bytes 2097168 | tf_op jit(solution)/shard_map/all_gather | solution.py:62
  173.5 3.1 fusion.17
  176.6 7.5 %all-to-all-start.4 = ((f32[16,32,256]{2,1,0:T(8,128)}), f32[16,32,256]{2,1,0:T(8,128)}, u32[]{:S(2)}, u32[]{:S(2)}) async-start(f32[16,32,256]{2,1,0:T(8,128)} %bitcast.59), calls=%async_computation.4 | async-start | bytes 1048576 | tf_op jit(solution)/shard_map/all_to_all | solution.py:41
  184.2 75.2 %all-gather.5.cloned.1.call-done = bf16[2048,512]{1,0:T(8,128)(2,1)} async-done(((bf16[64,512]{1,0:T(8,128)(2,1)}), bf16[2048,512]{1,0:T(8,128)(2,1)}) %all-gather.5.cloned.1.call-update) | async-done | bytes 2097168 | tf_op jit(solution)/shard_map/all_gather | solution.py:62
  259.4 3.1 fusion.16
  262.6 8.9 %all-to-all-start.1 = ((f32[16,32,256]{2,1,0:T(8,128)}), f32[16,32,256]{2,1,0:T(8,128)}, u32[]{:S(2)}, u32[]{:S(2)}) async-start(f32[16,32,256]{2,1,0:T(8,128)} %bitcast.58), calls=%async_computation.1 | async-start | bytes 1048576 | tf_op jit(solution)/shard_map/all_to_all | solution.py:41
  271.4 1.1 reduce_sum.19
  272.5 13.9 %all-to-all-done.1 = f32[16,32,256]{2,1,0:T(8,128)} async-done(((f32[16,32,256]{2,1,0:T(8,128)}), f32[16,32,256]{2,1,0:T(8,128)}, u32[]{:S(2)}, u32[]{:S(2)}) %all-to-all-start.1) | async-done | bytes 524320 | tf_op jit(solution)/shard_map/all_to_all | solution.py:41
  286.4 1.1 reduce_sum.18
  287.5 0.1 fusion.10
  287.6 15.1 %all_to_all.32 = bf16[16,32,256]{2,1,0:T(8,128)(2,1)} all-to-all(bf16[16,32,256]{2,1,0:T(8,128)(2,1)S(1)} %broadcast_in_dim.35), channel_id=1, replica_groups=mesh['dp'=16,'fsdp'=32] {'dp'}, dimensions={0} | all-to-all | bytes 524288 | tf_op jit(solution)/shard_map/all_to_all | solution.py:20
  302.8 0.7 broadcast_in_dim.39
  303.5 5.3 %all-to-all-start.5 = ((bf16[16,32,256]{2,1,0:T(8,128)(2,1)}), bf16[16,32,256]{2,1,0:T(8,128)(2,1)S(1)}, u32[]{:S(2)}, u32[]{:S(2)}) async-start(bf16[16,32,256]{2,1,0:T(8,128)(2,1)} %broadcast_in_dim.39), calls=%async_computation.5 | async-start | bytes 524288 | tf_op jit(solution)/shard_map/all_to_all | solution.py:20
  308.8 0.7 pad_maximum_fusion.1
  309.4 1.2 fusion.2
  310.7 7.3 %all-to-all-done.5 = bf16[16,32,256]{2,1,0:T(8,128)(2,1)S(1)} async-done(((bf16[16,32,256]{2,1,0:T(8,128)(2,1)}), bf16[16,32,256]{2,1,0:T(8,128)(2,1)S(1)}, u32[]{:S(2)}, u32[]{:S(2)}) %all-to-all-start.5) | async-done | bytes 262176 | tf_op jit(solution)/shard_map/all_to_all | solution.py:20
  317.9 0.3 fusion.3
  318.2 0.6 pad_maximum_fusion
  (12 shorter events, 0.1 us)
Async XLA Ops:
  7.2 166.3 %copy-start = (bf16[2048,256]{1,0:T(8,128)(2,1)S(1)}, bf16[2048,256]{1,0:T(8,128)(2,1)}, u32[]{:S(2)}) copy-start(bf16[2048,256]{1,0:T(8,128)(2,1)} %param.6) | copy-start | bytes 3145732
  7.2 84.7 %copy-start.1 = (bf16[2,64,1024]{2,1,0:T(8,128)(2,1)S(1)}, bf16[2,64,1024]{2,1,0:T(8,128)(2,1)}, u32[]{:S(2)}) copy-start(bf16[2,64,1024]{2,1,0:T(8,128)(2,1)} %param.7) | copy-start | bytes 786436
  7.2 166.3 %all-gather.7.cloned.1.call-start = ((), (), s32[]{:S(2)}) async-start(), calls=%async_computation.7 | async-start | bytes 2162688 | tf_op jit(solution)/shard_map/all_gather | solution.py:62
  93.0 166.4 %all-gather.5.cloned.1.call-start = ((), (), s32[]{:S(2)}) async-start(), calls=%async_computation.6 | async-start | bytes 2162688 | tf_op jit(solution)/shard_map/all_gather | solution.py:62
  176.6 85.9 %all-to-all-start.4 = ((f32[16,32,256]{2,1,0:T(8,128)}), f32[16,32,256]{2,1,0:T(8,128)}, u32[]{:S(2)}, u32[]{:S(2)}) async-start(f32[16,32,256]{2,1,0:T(8,128)} %bitcast.59), calls=%async_computation.4 | async-start | bytes 1048576 | tf_op jit(solution)/shard_map/all_to_all | solution.py:41
  184.2 103.3 %copy-start.2 = (f32[2,32,256]{2,1,0:T(8,128)S(1)}, f32[2,32,256]{2,1,0:T(8,128)}, u32[]{:S(2)}) copy-start(f32[2,32,256]{2,1,0:T(8,128)} %param.9) | copy-start | bytes 196612
  184.2 103.3 %copy-start.3 = (f32[2,32,256]{2,1,0:T(8,128)S(1)}, f32[2,32,256]{2,1,0:T(8,128)}, u32[]{:S(2)}) copy-start(f32[2,32,256]{2,1,0:T(8,128)} %param.10) | copy-start | bytes 196612
  262.6 23.9 %all-to-all-start.1 = ((f32[16,32,256]{2,1,0:T(8,128)}), f32[16,32,256]{2,1,0:T(8,128)}, u32[]{:S(2)}, u32[]{:S(2)}) async-start(f32[16,32,256]{2,1,0:T(8,128)} %bitcast.58), calls=%async_computation.1 | async-start | bytes 1048576 | tf_op jit(solution)/shard_map/all_to_all | solution.py:41
  303.5 14.5 %all-to-all-start.5 = ((bf16[16,32,256]{2,1,0:T(8,128)(2,1)}), bf16[16,32,256]{2,1,0:T(8,128)(2,1)S(1)}, u32[]{:S(2)}, u32[]{:S(2)}) async-start(bf16[16,32,256]{2,1,0:T(8,128)(2,1)} %broadcast_in_dim.39), calls=%async_computation.5 | async-start | bytes 524288 | tf_op jit(solution)/shard_map/all_to_all | solution.py:20
Sparse Core Ops, SparseCore 0:
  93.1 80.3 all-gather.6
  177.4 81.9 all-gather.4
where the time goes:
time: 327 us; the launch traced here: 326 us
  blocking collectives  166 us (51%)
  waiting for transfers between devices  103 us (31%)
  starting transfers between devices  21.8 us (7%)
  between operations  18 us (6%)
  matrix products  9.98 us (3%)
  other arithmetic  3.52 us (1%)
    all_to_all x3, blocking collectives, sent_to_all(): lax.all_to_all(jnp.broadcast_to(x[None], (count, *x.shape)), axis, 0, 0,...  91.5 us
    all_gather x2, waiting for transfers between devices, on_device(): lax.all_gather(head_rows, 'fsdp', axis=0, tiled=True)  82.2 us
    all_gather x2, blocking collectives, broadcast(): lax.all_gather(x, axis)  74.3 us
    all_to_all x2, starting transfers between devices, summed_on_arrival(): lax.all_to_all(blocks, axis, split_axis=0, concat_axis=0, tiled=True)  16.4 us
    all_to_all x2, waiting for transfers between devices, summed_on_arrival(): lax.all_to_all(blocks, axis, split_axis=0, concat_axis=0, tiled=True)  14 us
    all_to_all x1, waiting for transfers between devices, sent_to_all(): lax.all_to_all(jnp.broadcast_to(x[None], (count, *x.shape)), axis, 0, 0,...  7.26 us
  transfers between devices with their start and end apart: 5, of which 4 were waited for; matrix products, arithmetic and copies ran while one was open for 3% of the time, Pallas kernels for 0%

commit v1 on v0

--- a/solution.py
+++ b/solution.py
@@ -59,7 +59,9 @@
             cotangent[matrix], projector, preferred_element_type=jnp.float32
         ).astype(jnp.bfloat16)
         partial_value = lax.dot_general(
-            lax.all_gather(head_rows, "fsdp", axis=0, tiled=True),
+            jnp.concatenate(
+                lax.all_to_all(jnp.stack([head_rows] * lax.axis_size("fsdp")), "fsdp", 0, 0), axis=0
+            ),
             layer_input,
             (((0,), (0,)), ((), ())),
             preferred_element_type=jnp.float32,

time: 327 us -> 322 us (0.985)
  the two profiles are of different devices: /device:TPU:2 before, /device:TPU:8 now
where the time goes in v1:
time: 322 us; the launch traced here: 321 us
  waiting for transfers between devices  158 us (49%)
  blocking collectives  90.1 us (28%)
  starting transfers between devices  39.7 us (12%)
  local copies, waits for them, and re-layouts  15.3 us (5%)
  matrix products  10.7 us (3%)
  between operations  4.73 us (1%)
    all_to_all x2, waiting for transfers between devices, on_device(): lax.all_to_all(jnp.stack([head_rows] * lax.axis_size('fsdp')), 'fsdp', 0, 0)  96.5 us
    all_gather x2, blocking collectives, broadcast(): lax.all_gather(x, axis)  76.2 us
    all_to_all x3, waiting for transfers between devices, sent_to_all(): lax.all_to_all(jnp.broadcast_to(x[None], (count, *x.shape)), axis, 0, 0,...  37.3 us
    all_to_all x2, waiting for transfers between devices, summed_on_arrival(): lax.all_to_all(blocks, axis, split_axis=0, concat_axis=0, tiled=True)  23.9 us
    all_to_all x3, starting transfers between devices, sent_to_all(): lax.all_to_all(jnp.broadcast_to(x[None], (count, *x.shape)), axis, 0, 0,...  23.4 us
    all_to_all x1, blocking collectives, sent_to_all(): lax.all_to_all(jnp.broadcast_to(x[None], (count, *x.shape)), axis, 0, 0,...  14 us
    all_to_all x2, starting transfers between devices, summed_on_arrival(): lax.all_to_all(blocks, axis, split_axis=0, concat_axis=0, tiled=True)  8.76 us
    all_to_all x2, starting transfers between devices, on_device(): lax.all_to_all(jnp.stack([head_rows] * lax.axis_size('fsdp')), 'fsdp', 0, 0)  7.6 us
  transfers between devices with their start and end apart: 7, of which 6 were waited for; matrix products, arithmetic and copies ran while one was open for 6% of the time, Pallas kernels for 0%

profile of v1, /device:TPU:8, one launch (start us, length us, event | category | flops | bytes accessed | tf_op | source)
XLA Modules:
  0.0 320.9 jit_solution(16991067721166193075)
XLA Ops:
  0.6 1.3 fusion.19
  3.3 0.8 fusion.18
  4.1 42.3 %all-gather.1 = bf16[16,1,1024,16]{2,3,1,0:T(8,128)(2,1)S(1)} all-gather(bf16[1,1,1024,16]{2,3,1,0:T(8,128)(2,1)S(1)} %get-tuple-element.13), channel_id=3, replica_groups=mesh['dp'=16,'fsdp'=32] {'dp'}, dimensions={0}, use_global_device_ids=true | all-gather | bytes 557056 | tf_op jit(solution)/shard_map/all_gather | solution.py:15
  47.0 1.1 broadcast_in_dim.37
  48.1 9.9 %all-to-all-start.4 = ((bf16[32,1024,16]{1,2,0:T(8,128)(2,1)}), bf16[32,1024,16]{1,2,0:T(8,128)(2,1)S(1)}, u32[]{:S(2)}, u32[]{:S(2)}) async-start(bf16[32,1024,16]{1,2,0:T(8,128)(2,1)} %broadcast_in_dim.37), calls=%async_computation.4 | async-start | bytes 2097152 | tf_op jit(solution)/shard_map/all_to_all | solution.py:20
  60.0 33.9 %all-gather = bf16[16,1,1024,16]{2,3,1,0:T(8,128)(2,1)S(1)} all-gather(bf16[1,1,1024,16]{2,3,1,0:T(8,128)(2,1)S(1)} %get-tuple-element.12), channel_id=2, replica_groups=mesh['dp'=16,'fsdp'=32] {'dp'}, dimensions={0}, use_global_device_ids=true | all-gather | bytes 557056 | tf_op jit(solution)/shard_map/all_gather | solution.py:15
  93.9 1.3 broadcast_in_dim.33
  95.2 9.2 %all-to-all-start = ((bf16[32,1024,16]{1,2,0:T(8,128)(2,1)}), bf16[32,1024,16]{1,2,0:T(8,128)(2,1)S(1)}, u32[]{:S(2)}, u32[]{:S(2)}) async-start(bf16[32,1024,16]{1,2,0:T(8,128)(2,1)} %broadcast_in_dim.33), calls=%async_computation | async-start | bytes 2097152 | tf_op jit(solution)/shard_map/all_to_all | solution.py:20
  104.8 30.0 %all-to-all-done = bf16[32,1024,16]{1,2,0:T(8,128)(2,1)S(1)} async-done(((bf16[32,1024,16]{1,2,0:T(8,128)(2,1)}), bf16[32,1024,16]{1,2,0:T(8,128)(2,1)S(1)}, u32[]{:S(2)}, u32[]{:S(2)}) %all-to-all-start) | async-done | bytes 1048608 | tf_op jit(solution)/shard_map/all_to_all | solution.py:20
  134.8 1.7 stack.16
  136.5 3.8 %all-to-all-start.5 = ((bf16[32,64,512]{2,1,0:T(8,128)(2,1)}), bf16[32,64,512]{2,1,0:T(8,128)(2,1)S(1)}, u32[]{:S(2)}, u32[]{:S(2)}) async-start(bf16[32,64,512]{2,1,0:T(8,128)(2,1)} %stack.16), calls=%async_computation.5 | async-start | bytes 4194304 | tf_op jit(solution)/shard_map/all_to_all | solution.py:63
  140.3 1.7 fusion
  142.0 51.0 %all-to-all-done.5 = bf16[32,64,512]{2,1,0:T(8,128)(2,1)S(1)} async-done(((bf16[32,64,512]{2,1,0:T(8,128)(2,1)}), bf16[32,64,512]{2,1,0:T(8,128)(2,1)S(1)}, u32[]{:S(2)}, u32[]{:S(2)}) %all-to-all-start.5) | async-done | bytes 2097184 | tf_op jit(solution)/shard_map/all_to_all | solution.py:63
  193.0 1.7 stack.14
  194.9 3.8 %all-to-all-start.1 = ((bf16[32,64,512]{2,1,0:T(8,128)(2,1)}), bf16[32,64,512]{2,1,0:T(8,128)(2,1)S(1)}, u32[]{:S(2)}, u32[]{:S(2)}) async-start(bf16[32,64,512]{2,1,0:T(8,128)(2,1)} %stack.14), calls=%async_computation.1 | async-start | bytes 4194304 | tf_op jit(solution)/shard_map/all_to_all | solution.py:63
  198.8 4.0 %copy.14 = bf16[512,2048]{1,0:T(8,128)(2,1)} copy(bf16[512,2048]{0,1:T(8,128)(2,1)} %bitcast.64) | data formatting | bytes 4194304 | tf_op jit(solution)/shard_map/dot_general | solution.py:61
  202.7 3.1 fusion.4
  205.8 45.5 %all-to-all-done.1 = bf16[32,64,512]{2,1,0:T(8,128)(2,1)S(1)} async-done(((bf16[32,64,512]{2,1,0:T(8,128)(2,1)}), bf16[32,64,512]{2,1,0:T(8,128)(2,1)S(1)}, u32[]{:S(2)}, u32[]{:S(2)}) %all-to-all-start.1) | async-done | bytes 2097184 | tf_op jit(solution)/shard_map/all_to_all | solution.py:63
  251.4 4.2 %all-to-all-start.6 = ((f32[16,32,256]{2,1,0:T(8,128)}), f32[16,32,256]{2,1,0:T(8,128)}, u32[]{:S(2)}, u32[]{:S(2)}) async-start(f32[16,32,256]{2,1,0:T(8,128)} %fusion.4), calls=%async_computation.6 | async-start | bytes 1048576 | tf_op jit(solution)/shard_map/all_to_all | solution.py:41
  255.6 2.5 copy.13
  258.1 3.1 fusion.6
  261.2 10.1 %all-to-all-done.6 = f32[16,32,256]{2,1,0:T(8,128)} async-done(((f32[16,32,256]{2,1,0:T(8,128)}), f32[16,32,256]{2,1,0:T(8,128)}, u32[]{:S(2)}, u32[]{:S(2)}) %all-to-all-start.6) | async-done | bytes 524320 | tf_op jit(solution)/shard_map/all_to_all | solution.py:41
  271.3 4.5 %all-to-all-start.2 = ((f32[16,32,256]{2,1,0:T(8,128)}), f32[16,32,256]{2,1,0:T(8,128)S(1)}, u32[]{:S(2)}, u32[]{:S(2)}) async-start(f32[16,32,256]{2,1,0:T(8,128)} %fusion.6), calls=%async_computation.2 | async-start | bytes 1048576 | tf_op jit(solution)/shard_map/all_to_all | solution.py:41
  275.8 1.1 reduce_sum.19
  276.9 13.8 %all-to-all-done.2 = f32[16,32,256]{2,1,0:T(8,128)S(1)} async-done(((f32[16,32,256]{2,1,0:T(8,128)}), f32[16,32,256]{2,1,0:T(8,128)S(1)}, u32[]{:S(2)}, u32[]{:S(2)}) %all-to-all-start.2) | async-done | bytes 524320 | tf_op jit(solution)/shard_map/all_to_all | solution.py:41
  290.9 14.0 %all_to_all.40 = bf16[16,32,256]{2,1,0:T(8,128)(2,1)S(1)} all-to-all(bf16[16,32,256]{2,1,0:T(8,128)(2,1)S(1)} %broadcast_in_dim.35), channel_id=1, replica_groups=mesh['dp'=16,'fsdp'=32] {'dp'}, dimensions={0} | all-to-all | bytes 524288 | tf_op jit(solution)/shard_map/all_to_all | solution.py:20
  304.9 0.7 broadcast_in_dim.39
  305.6 4.3 %all-to-all-start.7 = ((bf16[16,32,256]{2,1,0:T(8,128)(2,1)}), bf16[16,32,256]{2,1,0:T(8,128)(2,1)S(1)}, u32[]{:S(2)}, u32[]{:S(2)}) async-start(bf16[16,32,256]{2,1,0:T(8,128)(2,1)} %broadcast_in_dim.39), calls=%async_computation.7 | async-start | bytes 524288 | tf_op jit(solution)/shard_map/all_to_all | solution.py:20
  309.9 0.7 pad_maximum_fusion.1
  310.6 1.2 fusion.2
  311.7 7.3 %all-to-all-done.7 = bf16[16,32,256]{2,1,0:T(8,128)(2,1)S(1)} async-done(((bf16[16,32,256]{2,1,0:T(8,128)(2,1)}), bf16[16,32,256]{2,1,0:T(8,128)(2,1)S(1)}, u32[]{:S(2)}, u32[]{:S(2)}) %all-to-all-start.7) | async-done | bytes 262176 | tf_op jit(solution)/shard_map/all_to_all | solution.py:20
  319.0 1.2 fusion.3
  (22 shorter events, 1.5 us)
Async XLA Ops:
  0.6 202.1 %copy-start = (bf16[2048,256]{1,0:T(8,128)(2,1)S(1)}, bf16[2048,256]{1,0:T(8,128)(2,1)}, u32[]{:S(2)}) copy-start(bf16[2048,256]{1,0:T(8,128)(2,1)} %param.6) | copy-start | bytes 3145732
  48.1 45.8 %all-to-all-start.4 = ((bf16[32,1024,16]{1,2,0:T(8,128)(2,1)}), bf16[32,1024,16]{1,2,0:T(8,128)(2,1)S(1)}, u32[]{:S(2)}, u32[]{:S(2)}) async-start(bf16[32,1024,16]{1,2,0:T(8,128)(2,1)} %broadcast_in_dim.37), calls=%async_computation.4 | async-start | bytes 2097152 | tf_op jit(solution)/shard_map/all_to_all | solution.py:20
  58.0 46.4 %copy-start.4 = (bf16[2,64,1024]{2,1,0:T(8,128)(2,1)S(1)}, bf16[2,64,1024]{2,1,0:T(8,128)(2,1)}, u32[]{:S(2)}) copy-start(bf16[2,64,1024]{2,1,0:T(8,128)(2,1)} %param.7) | copy-start | bytes 786436
  93.9 10.9 %copy-start.2 = (bf16[32,1024,16]{1,2,0:T(8,128)(2,1)}, bf16[32,1024,16]{1,2,0:T(8,128)(2,1)S(1)}, u32[]{:S(2)}) copy-start(bf16[32,1024,16]{1,2,0:T(8,128)(2,1)S(1)} %all-to-all-done.4) | copy-start | bytes 3145732
  95.2 39.7 %all-to-all-start = ((bf16[32,1024,16]{1,2,0:T(8,128)(2,1)}), bf16[32,1024,16]{1,2,0:T(8,128)(2,1)S(1)}, u32[]{:S(2)}, u32[]{:S(2)}) async-start(bf16[32,1024,16]{1,2,0:T(8,128)(2,1)} %broadcast_in_dim.33), calls=%async_computation | async-start | bytes 2097152 | tf_op jit(solution)/shard_map/all_to_all | solution.py:20
  134.8 1.7 copy-start.3
  136.5 56.5 %all-to-all-start.5 = ((bf16[32,64,512]{2,1,0:T(8,128)(2,1)}), bf16[32,64,512]{2,1,0:T(8,128)(2,1)S(1)}, u32[]{:S(2)}, u32[]{:S(2)}) async-start(bf16[32,64,512]{2,1,0:T(8,128)(2,1)} %stack.16), calls=%async_computation.5 | async-start | bytes 4194304 | tf_op jit(solution)/shard_map/all_to_all | solution.py:63
  193.0 2.0 copy-start.1
  194.9 56.4 %all-to-all-start.1 = ((bf16[32,64,512]{2,1,0:T(8,128)(2,1)}), bf16[32,64,512]{2,1,0:T(8,128)(2,1)S(1)}, u32[]{:S(2)}, u32[]{:S(2)}) async-start(bf16[32,64,512]{2,1,0:T(8,128)(2,1)} %stack.14), calls=%async_computation.1 | async-start | bytes 4194304 | tf_op jit(solution)/shard_map/all_to_all | solution.py:63
  251.4 20.0 %all-to-all-start.6 = ((f32[16,32,256]{2,1,0:T(8,128)}), f32[16,32,256]{2,1,0:T(8,128)}, u32[]{:S(2)}, u32[]{:S(2)}) async-start(f32[16,32,256]{2,1,0:T(8,128)} %fusion.4), calls=%async_computation.6 | async-start | bytes 1048576 | tf_op jit(solution)/shard_map/all_to_all | solution.py:41
  258.1 32.7 %copy-start.5 = (f32[2,32,256]{2,1,0:T(8,128)S(1)}, f32[2,32,256]{2,1,0:T(8,128)}, u32[]{:S(2)}) copy-start(f32[2,32,256]{2,1,0:T(8,128)} %param.9) | copy-start | bytes 196612
  258.1 32.7 %copy-start.6 = (f32[2,32,256]{2,1,0:T(8,128)S(1)}, f32[2,32,256]{2,1,0:T(8,128)}, u32[]{:S(2)}) copy-start(f32[2,32,256]{2,1,0:T(8,128)} %param.10) | copy-start | bytes 196612
  271.3 19.4 %all-to-all-start.2 = ((f32[16,32,256]{2,1,0:T(8,128)}), f32[16,32,256]{2,1,0:T(8,128)S(1)}, u32[]{:S(2)}, u32[]{:S(2)}) async-start(f32[16,32,256]{2,1,0:T(8,128)} %fusion.6), calls=%async_computation.2 | async-start | bytes 1048576 | tf_op jit(solution)/shard_map/all_to_all | solution.py:41
  305.6 13.4 %all-to-all-start.7 = ((bf16[16,32,256]{2,1,0:T(8,128)(2,1)}), bf16[16,32,256]{2,1,0:T(8,128)(2,1)S(1)}, u32[]{:S(2)}, u32[]{:S(2)}) async-start(bf16[16,32,256]{2,1,0:T(8,128)(2,1)} %broadcast_in_dim.39), calls=%async_computation.7 | async-start | bytes 524288 | tf_op jit(solution)/shard_map/all_to_all | solution.py:20
